TPU v7x, 256 devices: a whole 4x4x8 slice. The times are simulated.
256 devices in a mesh: aux: 32 (over y, x, core), orb: 8 (over z).
Axes of the slice: x: 4, y: 4, z: 8, core: 2. Of those that a mesh axis runs over, the one named last changes fastest.
Arguments:
- band_pattern: int32 [256, 8], P('aux'), may hold values 0 or 1
- density_in: bfloat16 [256, 8, 128, 128], P('aux', 'orb')
- field_terms: bfloat16 [2, 256, 8, 128, 128], P(None, 'aux', 'orb'), may hold values from -3 to 3
- fit_blocks: int32 [1], replicated, may hold values from 0 to 255
- tensor: bfloat16 [1, 3072, 8, 16384], P(None, 'aux', 'orb'), may hold values from -0.015625 to 0.015625
- metric_inv: float32 [1, 3072, 3072], P(None, 'aux')
Outputs:
- response: bfloat16 [2, 256, 8, 128, 128], P(None, 'aux', 'orb')
- coefficients: float32 [1, 2, 3072], P(None, None, 'aux')
All inputs are finite; a program needn't handle non-finite values. No bound on the sum of `band_pattern` on one device may be relied on, other than what follows from the above.
Results may differ from a plain program's by a relative error of at most 0.0055.
Values may be sent and summed in bfloat16 or wider, within the bound.
A program may use at most 192 MiB of HBM per device.

v0:
```python
import jax
import jax.numpy as jnp
from jax import lax
from jax.sharding import PartitionSpec as P


def padded_2(block, sides, width):
    for axis, dim in sides:
        count = lax.axis_size(axis)
        forward = [(i, i + 1) for i in range(count - 1)]
        backward = [(target, source) for source, target in forward]
        low = lax.ppermute(
            lax.slice_in_dim(block, block.shape[dim] - width, None, axis=dim), axis, forward
        )
        high = lax.ppermute(lax.slice_in_dim(block, 0, width, axis=dim), axis, backward)
        block = jnp.concatenate([low, block, high], axis=dim)
    return block


def sent_to_all(x, axis):
    copies = jnp.broadcast_to(x, (lax.axis_size(axis), *x.shape))
    return lax.all_to_all(copies, axis, split_axis=0, concat_axis=0, tiled=True)


def over_copies(x, axis):
    everything = sent_to_all(x, axis)
    return jnp.sum(everything.astype(jnp.float32), axis=0)


def over_copies_2(x, axis):
    everything = sent_to_all(x, axis)
    return jnp.sum(everything, axis=0)


def joined_along(pieces, dim):
    pieces = jnp.moveaxis(pieces, 0, dim)
    lengths = pieces.shape
    return pieces.reshape(*lengths[:dim], lengths[dim] * lengths[dim + 1], *lengths[dim + 2 :])


def gathered_copies(x, axis, dim):
    pieces = sent_to_all(x, axis)
    return joined_along(pieces, dim)


def slide_slots(blocks, offset):
    slot_count = blocks.shape[2]
    if offset >= 0:
        padded = jnp.pad(blocks, ((0, 0), (0, 0), (offset, 0), (0, 0), (0, 0)))
        return padded[:, :, :slot_count]
    padded = jnp.pad(blocks, ((0, 0), (0, 0), (0, -offset), (0, 0), (0, 0)))
    return padded[:, :, -offset : -offset + slot_count]


def band_keep(band_pattern, first_row, total_rows):
    slot_count = band_pattern.shape[1]
    half_band = slot_count // 2
    row_ids = first_row + jnp.arange(band_pattern.shape[0], dtype=jnp.int32)[:, None]
    columns = row_ids + jnp.arange(slot_count, dtype=jnp.int32)[None, :] - half_band
    return (band_pattern == 1) & (columns >= 0) & (columns < total_rows)


def own_slot_product(factor_left, right_rims, my_slot):
    count_rows = factor_left.shape[1]
    slot_count = factor_left.shape[2]
    half_band = slot_count // 2
    lead_count = right_rims.shape[0]
    total = None
    for stride in range(slot_count):
        source_slot = my_slot - stride + half_band
        inside = (source_slot >= 0) & (source_slot < slot_count)
        starts = (
            jnp.int32(0),
            jnp.int32(stride),
            jnp.clip(source_slot, 0, slot_count - 1),
            jnp.int32(0),
            jnp.int32(0),
        )
        sizes = (lead_count, count_rows, 1, right_rims.shape[3], right_rims.shape[4])
        picked = lax.dynamic_slice(right_rims, starts, sizes)[:, :, 0]
        picked = jnp.where(inside, picked, jnp.zeros((), picked.dtype))
        product = jnp.matmul(factor_left[:, :, stride], picked, preferred_element_type=jnp.float32)
        total = product if total is None else total + product
    return total


def all_slot_product(factor_left, right_rims):
    count_rows = factor_left.shape[1]
    slot_count = factor_left.shape[2]
    half_band = slot_count // 2
    total = None
    for stride in range(slot_count):
        source = slide_slots(right_rims[:, stride : stride + count_rows], stride - half_band)
        product = jnp.matmul(
            factor_left[:, :, stride : stride + 1], source, preferred_element_type=jnp.float32
        )
        total = product if total is None else total + product
    return total


def rim_fields(field_rows, half_band):
    return padded_2(field_rows, (("aux", 1),), half_band)


def on_device(band_pattern, density_in, field_terms, fit_blocks, tensor, metric_inv):
    count_rows = density_in.shape[0]
    slot_count = lax.axis_size("orb")
    half_band = slot_count // 2
    total_rows = count_rows * lax.axis_size("aux")
    first_row = lax.axis_index("aux") * count_rows
    my_slot = lax.axis_index("orb")
    keep_all = band_keep(band_pattern, first_row, total_rows)
    keep_own = lax.dynamic_index_in_dim(keep_all, my_slot, 1, keepdims=True)[None, :, :, None, None]
    keep_out = keep_own[:, :, 0]
    zero_half = jnp.zeros((), jnp.bfloat16)
    density = jnp.where(keep_own, density_in[None], zero_half)
    perturbed = jnp.where(keep_own, field_terms, zero_half)
    stacked = jnp.concatenate([density, perturbed], 0)
    whole_rows = lax.all_gather(stacked, "orb", axis=2, tiled=True)
    deep_rows = padded_2(whole_rows[0:1], (("aux", 1),), 2 * half_band)
    field_rows = rim_fields(whole_rows[1:], half_band)
    pattern_wide = padded_2(band_pattern, (("aux", 0),), half_band)
    keep_wide = band_keep(pattern_wide, first_row - half_band, total_rows)[None, :, :, None, None]
    density_rims = deep_rows[:, half_band : half_band + count_rows + 2 * half_band]
    cross_term = own_slot_product(whole_rows[0:1], field_rows, my_slot)
    right_term = own_slot_product(whole_rows[1:], density_rims, my_slot)
    first_order = jnp.where(keep_out, cross_term + right_term, 0.0).astype(jnp.bfloat16)
    square_wide = all_slot_product(density_rims, deep_rows)
    square_rims = jnp.where(keep_wide, square_wide, 0.0).astype(jnp.bfloat16)
    square_rows = square_rims[:, half_band : half_band + count_rows]
    order_rows = lax.all_gather(first_order[:, :, None], "orb", axis=2, tiled=True)
    order_rims = rim_fields(order_rows, half_band)
    second = own_slot_product(square_rows, order_rims, my_slot) + own_slot_product(
        order_rows, square_rims, my_slot
    )
    response = jnp.where(keep_out, 2.0 * first_order.astype(jnp.float32) - second, 0.0).astype(
        jnp.bfloat16
    )[:, :, None]
    owner_row = fit_blocks // count_rows
    local_row = fit_blocks % count_rows
    own_piece = jnp.take(response, local_row, axis=1)
    owner_flag = (owner_row == lax.axis_index("aux"))[None, :, None, None, None]
    contrib = jnp.where(owner_flag, own_piece, zero_half).astype(jnp.float32)
    fitted = (
        over_copies(contrib.astype(jnp.bfloat16), "aux").astype(jnp.float32).astype(jnp.bfloat16)
    )
    flat_blocks = fitted.reshape(fitted.shape[0], fitted.shape[1], -1)
    integrals = tensor.reshape(tensor.shape[0], tensor.shape[1], -1)
    partial_value = jnp.einsum(
        "kfm,fpm->fkp", flat_blocks, integrals, preferred_element_type=jnp.float32
    )
    summed = over_copies_2(partial_value, "orb")
    full_sums = gathered_copies(summed, "aux", 2)
    coefficients = jnp.einsum(
        "fpq,fkq->fkp", metric_inv, full_sums, precision=lax.Precision.HIGHEST
    )
    return (response, coefficients)


def solution(mesh):
    in_specs = (
        P("aux", None),
        P("aux", "orb", None, None),
        P(None, "aux", "orb", None, None),
        P(),
        P(None, "aux", "orb", None),
        P(None, "aux", None),
    )
    out_specs = (P(None, "aux", "orb", None, None), P(None, None, "aux"))
    return jax.shard_map(
        on_device, mesh=mesh, in_specs=in_specs, out_specs=out_specs, check_vma=False
    )
```

profile of v0, /device:TPU:1, one launch (start us, length us, event | category | flops | bytes accessed | tf_op | source)
XLA Modules:
  0.0 341.7 jit_solution(3902713181150019706)
XLA Ops:
  8.3 1.1 copy_select_fusion
  9.5 1.0 bitcast_select_fusion
  11.6 78.4 %all-gather.4.cloned.1.call-done = bf16[3,8,8,128,128]{4,3,1,0,2:T(8,128)(2,1)} async-done(((bf16[3,8,1,128,128]{4,3,1,0,2:T(8,128)(2,1)}), bf16[3,8,8,128,128]{4,3,1,0,2:T(8,128)(2,1)}) %all-gather.4.cloned.1.call-update) | async-done | bytes 6291472 | tf_op jit(solution)/shard_map/all_gather | solution.py:119
  90.0 3.2 slice_bitcast_fusion
  93.2 3.6 %collective-permute-start.2 = (bf16[1,8,8,128,128]{4,3,0,1,2:T(8,128)(2,1)}, bf16[1,8,8,128,128]{4,3,0,1,2:T(8,128)(2,1)}, u32[]{:S(2)}, u32[]{:S(2)}) collective-permute-start(bf16[1,8,8,128,128]{4,3,0,1,2:T(8,128)(2,1)} %slice_bitcast_fusion), channel_id=1, source_target_pairs={{0,8},{8,16},{16,24},{24,32},{32,40},{40,48},{48,56},{56,64},{64,7... | collective-permute-start | bytes 6291464 | tf_op jit(solution)/shard_map/ppermute | solution.py:12
  96.9 2.0 collective-permute-start.3
  98.9 2.9 fusion.315
  101.8 1.6 copy.226
  103.4 3.6 %collective-permute-start = (bf16[2,4,8,128,128]{4,3,0,1,2:T(8,128)(2,1)}, bf16[2,4,8,128,128]{4,3,0,1,2:T(8,128)(2,1)}, u32[]{:S(2)}, u32[]{:S(2)}) collective-permute-start(bf16[2,4,8,128,128]{4,3,0,1,2:T(8,128)(2,1)} %copy.226), channel_id=1, source_target_pairs={{0,8},{8,16},{16,24},{24,32},{32,40},{40,48},{48,56},{56,64},{64,7... | collective-permute-start | bytes 6291464 | tf_op jit(solution)/shard_map/ppermute | solution.py:12
  107.1 2.1 collective-permute-start.1
  109.3 1.9 fusion.314
  111.2 8.9 %collective-permute-done.2 = bf16[1,8,8,128,128]{4,3,0,1,2:T(8,128)(2,1)} collective-permute-done((bf16[1,8,8,128,128]{4,3,0,1,2:T(8,128)(2,1)}, bf16[1,8,8,128,128]{4,3,0,1,2:T(8,128)(2,1)}, u32[]{:S(2)}, u32[]{:S(2)}) %collective-permute-start.2) | collective-permute-done | bytes 2097184 | tf_op jit(solution)/shard_map/ppermute | solution.py:12
  120.1 4.4 %collective-permute-done.3 = bf16[1,8,8,128,128]{4,3,0,1,2:T(8,128)(2,1)} collective-permute-done((bf16[1,8,8,128,128]{4,3,0,1,2:T(8,128)(2,1)}, bf16[1,8,8,128,128]{4,3,0,1,2:T(8,128)(2,1)}, u32[]{:S(2)}, u32[]{:S(2)}) %collective-permute-start.3) | collective-permute-done | bytes 2097184 | tf_op jit(solution)/shard_map/ppermute | solution.py:15
  124.5 3.7 %pad_maximum_fusion = bf16[1,24,8,128,128]{4,3,0,1,2:T(8,128)(2,1)S(1)} fusion(bf16[1,8,8,128,128]{4,3,0,1,2:T(8,128)(2,1)} %collective-permute-done.3, bf16[1,8,8,128,128]{4,3,0,1,2:T(8,128)(2,1)} %slice_bitcast_fusion, bf16[1,8,8,128,128]{4,3,0,1,2:T(8,128)(2,1)} %collective-permute-done.2), kind=kLoop, calls=%fused_computation.4 | loop fusion | flops 6291456 | bytes 12582912 | tf_op jit(solution)/shard_map/concatenate | solution.py:16
  128.2 11.0 %fusion.313 = (bf16[1,16,8,128,128]{4,3,0,1,2:T(8,128)(2,1)}, bf16[16,8,128,128]{3,2,0,1:T(8,128)(2,1)}, bf16[1,16,8,128,128]{4,3,0,1,2:T(8,128)(2,1)}, bf16[1,1...) fusion(bf16[1,24,8,128,128]{4,3,0,1,2:T(8,128)(2,1)S(1)} %pad_m, ...), kind=kLoop, calls=%fused_computation.404 | loop fusion | bytes 62914560 | tf_op jit(solution)/shard_map/slice | solution.py:93
  139.9 1.3 convolution_add_fusion.20
  141.3 1.3 collective-permute-done
  142.6 1.7 constant_dynamic-update-slice_fusion.1
  147.0 2.0 constant_dynamic-update-slice_fusion
  151.5 1.1 fusion.40
  152.7 4.0 %collective-permute-start.4 = (s32[4,8]{1,0:T(4,128)S(1)}, s32[4,8]{1,0:T(4,128)S(1)}, u32[]{:S(2)}, u32[]{:S(2)}) collective-permute-start(s32[4,8]{1,0:T(4,128)S(1)} %get-tuple-element.43), channel_id=1, source_target_pairs={{0,8},{8,16},{16,24},{24,32},{32,40},{40,48},{48,56},{56,64},{64,7... | collective-permute-start | bytes 392 | tf_op jit(solution)/shard_map/ppermute | solution.py:12
  156.7 2.1 collective-permute-start.5
  159.5 2.1 collective-permute-done.5
  161.7 3.7 %fusion.4 = (bf16[16,8,128,128]{3,2,0,1:T(8,128)(2,1)S(1)}, bf16[16,8,128,128]{3,2,0,1:T(8,128)(2,1)S(1)}) fusion(bf16[1,16,8,128,128]{4,3,0,1,2:T(8,128)(2,1)} %get-tuple-element.28, bf16[1,16,8,128,128]{4,3,0,1,2:T(8,128)(2,1)} %get-tuple-element.25), kind=kLoop, calls=%fused_computation.13 | loop fusion | bytes 16777216 | tf_op jit(solution)/shard_map/squeeze | solution.py:94
  165.9 3.4 fusion.2
  169.3 1.0 slice-done.1
  170.3 4.3 %fusion.22 = f32[16,128,8,128]{3,1,2,0:T(8,128)} fusion(bf16[1,24,8,128,128]{4,3,0,1,2:T(8,128)(2,1)S(1)} %bitcast.473, bf16[1,16,8,128,128]{4,3,0,1,2:T(8,128)(2,1)S(1)} %copy-done.6), kind=kOutput, calls=%fused_computation.32 | convolution fusion | flops 536870912 | bytes 13107200 | tf_op jit(solution)/shard_map/dot_general | solution.py:94
  174.6 4.5 %fusion.12 = f32[16,128,8,128]{3,1,2,0:T(8,128)} fusion(bf16[16,8,128,128]{3,2,0,1:T(8,128)(2,1)S(1)} %get-tuple-element.48, bf16[1,24,8,128,128]{4,3,0,1,2:T(8,128)(2,1)S(1)} %bitcast.473), kind=kOutput, calls=%fused_computation.22 | convolution fusion | flops 536870912 | bytes 13107200 | tf_op jit(solution)/shard_map/dot_general | solution.py:94
  179.2 4.5 %fusion.14 = f32[16,128,8,128]{3,1,2,0:T(8,128)} fusion(bf16[16,8,128,128]{3,2,0,1:T(8,128)(2,1)S(1)} %get-tuple-element.46, bf16[1,24,8,128,128]{4,3,0,1,2:T(8,128)(2,1)S(1)} %bitcast.473), kind=kOutput, calls=%fused_computation.24 | convolution fusion | flops 536870912 | bytes 13107200 | tf_op jit(solution)/shard_map/dot_general | solution.py:94
  183.6 4.5 %fusion.18 = f32[16,128,8,128]{3,1,2,0:T(8,128)} fusion(bf16[16,8,128,128]{3,2,0,1:T(8,128)(2,1)S(1)} %get-tuple-element.45, bf16[1,24,8,128,128]{4,3,0,1,2:T(8,128)(2,1)S(1)} %bitcast.473), kind=kOutput, calls=%fused_computation.28 | convolution fusion | flops 536870912 | bytes 13107200 | tf_op jit(solution)/shard_map/dot_general | solution.py:94
  188.2 4.5 %fusion.20 = f32[16,128,8,128]{3,1,2,0:T(8,128)} fusion(bf16[16,8,128,128]{3,2,0,1:T(8,128)(2,1)S(1)} %get-tuple-element.47, bf16[1,24,8,128,128]{4,3,0,1,2:T(8,128)(2,1)S(1)} %bitcast.473), kind=kOutput, calls=%fused_computation.30 | convolution fusion | flops 536870912 | bytes 13107200 | tf_op jit(solution)/shard_map/dot_general | solution.py:94
  192.7 4.5 %fusion.16 = f32[16,128,8,128]{3,1,2,0:T(8,128)} fusion(bf16[16,8,128,128]{3,2,0,1:T(8,128)(2,1)S(1)} %copy-done.5, bf16[1,24,8,128,128]{4,3,0,1,2:T(8,128)(2,1)S(1)} %bitcast.473), kind=kOutput, calls=%fused_computation.26 | convolution fusion | flops 536870912 | bytes 13107200 | tf_op jit(solution)/shard_map/dot_general | solution.py:94
  197.2 5.9 %fusion.24 = f32[16,128,8,128]{3,1,2,0:T(8,128)} fusion(bf16[1,24,8,128,128]{4,3,0,1,2:T(8,128)(2,1)S(1)} %bitcast.473, bf16[1,8,8,128,128]{4,3,0,1,2:T(8,128)(2,1)} %slice_bitcast_fusion, bf16[1,8,8,128,128]{4,3,0,1,2:T(8,128)(2,1)} %collective-permute-done.2), kind=kOutput, calls=%fused_computation.34 | convolution fusion | flops 553648128 | bytes 13107200 | tf_op jit(solution)/shard_map/dot_general | solution.py:94
  203.1 4.2 %all-gather.6.cloned.1.call-done = bf16[2,8,1024,128]{3,2,0,1:T(8,128)(2,1)} async-done(((bf16[2,8,128,128]{3,2,0,1:T(8,128)(2,1)}), bf16[2,8,1024,128]{3,2,0,1:T(8,128)(2,1)}) %all-gather.6.cloned.1.call-update) | async-done | bytes 4194320 | tf_op jit(solution)/shard_map/all_gather | solution.py:131
  207.2 5.1 %fusion.316 = (bf16[2,4,8,128,128]{4,3,0,1,2:T(8,128)(2,1)}, bf16[2,4,8,128,128]{4,3,0,1,2:T(8,128)(2,1)}) fusion(bf16[2,8,8,128,128]{4,3,2,0,1:T(8,128)(2,1)} %bitcast.476), kind=kLoop, calls=%fused_computation.407 | loop fusion | bytes 8388608 | tf_op jit(solution)/shard_map/slice | solution.py:15
  212.3 3.8 %collective-permute-start.6 = (bf16[2,4,8,128,128]{4,3,0,1,2:T(8,128)(2,1)}, bf16[2,4,8,128,128]{4,3,0,1,2:T(8,128)(2,1)S(1)}, u32[]{:S(2)}, u32[]{:S(2)}) collective-permute-start(bf16[2,4,8,128,128]{4,3,0,1,2:T(8,128)(2,1)} %get-tuple-element.42), channel_id=1, source_target_pairs={{0,8},{8,16},{16,24},{24,32},{32,40},{40,48},{48,56},{56,64},{64,7... | collective-permute-start | bytes 6291464 | tf_op jit(solution)/shard_map/ppermute | solution.py:12
  216.1 20.1 %select_convert_fusion = bf16[16,128,8,128]{3,1,2,0:T(8,128)(2,1)} fusion(f32[16,128,8,128]{3,1,2,0:T(8,128)} %fusion.12, f32[16,128,8,128]{3,1,2,0:T(8,128)} %fusion.14, f32[16,128,8,128]{3,1,2,0:T(8,128)} %fusion.16, f32[16,128,8,128]{3,1,2,0:T(8,128)} %fusion.18, f32[16,128,8,128]{3,1,2,0:T(8,128)S(1)} %copy-done.3, f32[16,128,8,128]{3,1,2,0:T(8,128)} %fusion.24, ...), kind=kOutput, calls=%fused_computation.3 | convolution fusion | flops 555745280 | bytes 67633280 | tf_op jit(solution)/shard_map/dot_general | solution.py:94
  236.2 2.4 collective-permute-start.7
  238.6 1.2 fusion.46
  239.9 1.2 convolution_add_fusion.6
  243.5 20.5 %collective-permute-done.7 = bf16[2,4,8,128,128]{4,3,0,1,2:T(8,128)(2,1)S(1)} collective-permute-done((bf16[2,4,8,128,128]{4,3,0,1,2:T(8,128)(2,1)}, bf16[2,4,8,128,128]{4,3,0,1,2:T(8,128)(2,1)S(1)}, u32[]{:S(2)}, u32[]{:S(2)}) %collective-permute-start.7) | collective-permute-done | bytes 2097184 | tf_op jit(solution)/shard_map/ppermute | solution.py:15
  268.6 36.8 %all_to_all.15 = bf16[32,2,1,1,128,128]{5,4,3,2,1,0:T(8,128)(2,1)} all-to-all(bf16[32,2,1,1,128,128]{5,4,3,2,1,0:T(8,128)(2,1)S(1)} %broadcast_in_dim.168), channel_id=1, replica_groups=mesh['aux'=32,'orb'=8] {'aux'}, dimensions={0} | all-to-all | bytes 4194304 | tf_op jit(solution)/shard_map/all_to_all | solution.py:22
  305.4 1.9 reduce_sum.21
  308.2 10.4 %all_to_all.16 = f32[8,1,2,96]{3,2,1,0:T(2,128)S(1)} all-to-all(f32[8,1,2,96]{3,2,1,0:T(2,128)S(1)} %broadcast_in_dim.169), channel_id=1, replica_groups=mesh['aux'=32,'orb'=8] {'orb'}, dimensions={0} | all-to-all | bytes 12288 | tf_op jit(solution)/shard_map/all_to_all | solution.py:22
  319.3 5.3 %all-to-all-start.2 = ((f32[32,1,2,96]{3,2,1,0:T(2,128)}), f32[32,1,2,96]{3,2,1,0:T(2,128)S(1)}, u32[]{:S(2)}, u32[]{:S(2)}) async-start(f32[32,1,2,96]{3,2,1,0:T(2,128)} %broadcast_in_dim.170), calls=%async_computation.2 | async-start | bytes 65536 | tf_op jit(solution)/shard_map/all_to_all | solution.py:22
  324.6 1.9 copy.172
  326.5 5.5 %all-to-all-done.2 = f32[32,1,2,96]{3,2,1,0:T(2,128)S(1)} async-done(((f32[32,1,2,96]{3,2,1,0:T(2,128)}), f32[32,1,2,96]{3,2,1,0:T(2,128)S(1)}, u32[]{:S(2)}, u32[]{:S(2)}) %all-to-all-start.2) | async-done | bytes 24608 | tf_op jit(solution)/shard_map/all_to_all | solution.py:22
  332.0 2.9 fusion.43
  (99 shorter events, 17.2 us)
Async XLA Ops:
  7.2 300.2 %copy-start = (bf16[1,96,1,16384]{3,1,2,0:T(8,128)(2,1)S(1)}, bf16[1,96,1,16384]{3,1,2,0:T(8,128)(2,1)}, u32[]{:S(2)}) copy-start(bf16[1,96,1,16384]{3,1,2,0:T(8,128)(2,1)} %param.10) | copy-start | bytes 9437188
  7.2 82.8 %all-gather.4.cloned.1.call-start = ((), (), s32[]{:S(2)}) async-start(), calls=%async_computation.3 | async-start | bytes 7077888 | tf_op jit(solution)/shard_map/all_gather | solution.py:119
  11.6 195.7 %all-gather.6.cloned.1.call-start = ((), (), s32[]{:S(2)}) async-start(), calls=%async_computation.4 | async-start | bytes 4718592 | tf_op jit(solution)/shard_map/all_gather | solution.py:131
  93.2 26.9 %collective-permute-start.2 = (bf16[1,8,8,128,128]{4,3,0,1,2:T(8,128)(2,1)}, bf16[1,8,8,128,128]{4,3,0,1,2:T(8,128)(2,1)}, u32[]{:S(2)}, u32[]{:S(2)}) collective-permute-start(bf16[1,8,8,128,128]{4,3,0,1,2:T(8,128)(2,1)} %slice_bitcast_fusion), channel_id=1, source_target_pairs={{0,8},{8,16},{16,24},{24,32},{32,40},{40,48},{48,56},{56,64},{64,7... | collective-permute-start | bytes 6291464 | tf_op jit(solution)/shard_map/ppermute | solution.py:12
  96.9 27.7 %collective-permute-start.3 = (bf16[1,8,8,128,128]{4,3,0,1,2:T(8,128)(2,1)}, bf16[1,8,8,128,128]{4,3,0,1,2:T(8,128)(2,1)}, u32[]{:S(2)}, u32[]{:S(2)}) collective-permute-start(bf16[1,8,8,128,128]{4,3,0,1,2:T(8,128)(2,1)} %slice_bitcast_fusion), channel_id=1, source_target_pairs={{8,0},{16,8},{24,16},{32,24},{40,32},{48,40},{56,48},{64,56},{72,6... | collective-permute-start | bytes 6291464 | tf_op jit(solution)/shard_map/ppermute | solution.py:15
  98.9 10.4 %slice-start.2 = ((s8[6291456]{0:T(1024)(128)(4,1)}), s8[4194304]{0:T(1024)(128)(4,1)S(1)}, s32[]{:S(2)}) async-start(s8[6291456]{0:T(1024)(128)(4,1)} %bitcast.474), calls=%async_computation.7 | async-start | bytes 8388608
  101.8 7.5 %slice-start.3 = ((s8[6291456]{0:T(1024)(128)(4,1)}), s8[2097152]{0:T(1024)(128)(4,1)S(1)}, s32[]{:S(2)}) async-start(s8[6291456]{0:T(1024)(128)(4,1)} %bitcast.474), calls=%async_computation.8 | async-start | bytes 4194304
  103.4 39.2 %collective-permute-start = (bf16[2,4,8,128,128]{4,3,0,1,2:T(8,128)(2,1)}, bf16[2,4,8,128,128]{4,3,0,1,2:T(8,128)(2,1)}, u32[]{:S(2)}, u32[]{:S(2)}) collective-permute-start(bf16[2,4,8,128,128]{4,3,0,1,2:T(8,128)(2,1)} %copy.226), channel_id=1, source_target_pairs={{0,8},{8,16},{16,24},{24,32},{32,40},{40,48},{48,56},{56,64},{64,7... | collective-permute-start | bytes 6291464 | tf_op jit(solution)/shard_map/ppermute | solution.py:12
  107.1 39.9 %collective-permute-start.1 = (bf16[2,4,8,128,128]{4,3,0,1,2:T(8,128)(2,1)S(1)}, bf16[2,4,8,128,128]{4,3,0,1,2:T(8,128)(2,1)}, u32[]{:S(2)}, u32[]{:S(2)}) collective-permute-start(bf16[2,4,8,128,128]{4,3,0,1,2:T(8,128)(2,1)S(1)} %copy.228), channel_id=1, source_target_pairs={{8,0},{16,8},{24,16},{32,24},{40,32},{48,40},{56,48},{64,56},{72,6... | collective-permute-start | bytes 6291464 | tf_op jit(solution)/shard_map/ppermute | solution.py:15
  128.2 11.5 %copy-start.1 = (bf16[1,24,8,128,128]{4,3,0,1,2:T(8,128)(2,1)}, bf16[1,24,8,128,128]{4,3,0,1,2:T(8,128)(2,1)S(1)}, u32[]{:S(2)}) copy-start(bf16[1,24,8,128,128]{4,3,0,1,2:T(8,128)(2,1)S(1)} %pad_maximum_fusion) | copy-start | bytes 18874372
  139.6 4.7 %copy-start.15 = (bf16[2,8,1,128,128]{4,3,1,0,2:T(8,128)(2,1)S(1)}, bf16[2,8,1,128,128]{4,3,1,0,2:T(8,128)(2,1)}, u32[]{:S(2)}) copy-start(bf16[2,8,1,128,128]{4,3,1,0,2:T(8,128)(2,1)} %get-tuple-element.35) | copy-start | bytes 1572868
  141.3 3.4 copy-start.14
  141.3 3.7 %copy-start.13 = (bf16[2,8,1,128,128]{4,3,1,0,2:T(8,128)(2,1)S(1)}, bf16[2,8,1,128,128]{4,3,1,0,2:T(8,128)(2,1)}, u32[]{:S(2)}) copy-start(bf16[2,8,1,128,128]{4,3,1,0,2:T(8,128)(2,1)} %get-tuple-element.33) | copy-start | bytes 1572868
  144.3 1.0 copy-start.12
  144.7 1.1 copy-start.11
  150.5 1.0 copy-start.10
  150.8 1.9 copy-start.16
  152.7 6.8 %collective-permute-start.4 = (s32[4,8]{1,0:T(4,128)S(1)}, s32[4,8]{1,0:T(4,128)S(1)}, u32[]{:S(2)}, u32[]{:S(2)}) collective-permute-start(s32[4,8]{1,0:T(4,128)S(1)} %get-tuple-element.43), channel_id=1, source_target_pairs={{0,8},{8,16},{16,24},{24,32},{32,40},{40,48},{48,56},{56,64},{64,7... | collective-permute-start | bytes 392 | tf_op jit(solution)/shard_map/ppermute | solution.py:12
  156.7 4.9 %collective-permute-start.5 = (s32[4,8]{1,0:T(4,128)S(1)}, s32[4,8]{1,0:T(4,128)S(1)}, u32[]{:S(2)}, u32[]{:S(2)}) collective-permute-start(s32[4,8]{1,0:T(4,128)S(1)} %get-tuple-element.44), channel_id=1, source_target_pairs={{8,0},{16,8},{24,16},{32,24},{40,32},{48,40},{56,48},{64,56},{72,6... | collective-permute-start | bytes 392 | tf_op jit(solution)/shard_map/ppermute | solution.py:15
  161.7 4.2 %copy-start.7 = (bf16[1,16,8,128,128]{4,3,0,1,2:T(8,128)(2,1)S(1)}, bf16[1,16,8,128,128]{4,3,0,1,2:T(8,128)(2,1)}, u32[]{:S(2)}) copy-start(bf16[1,16,8,128,128]{4,3,0,1,2:T(8,128)(2,1)} %get-tuple-element.26) | copy-start | bytes 12582916
  161.7 7.6 %slice-start = ((s8[6291456]{0:T(1024)(128)(4,1)}), s8[4194304]{0:T(1024)(128)(4,1)S(1)}, s32[]{:S(2)}) async-start(s8[6291456]{0:T(1024)(128)(4,1)} %bitcast.472), calls=%async_computation.5 | async-start | bytes 8388608
  165.4 4.9 %slice-start.1 = ((s8[6291456]{0:T(1024)(128)(4,1)}), s8[2097152]{0:T(1024)(128)(4,1)S(1)}, s32[]{:S(2)}) async-start(s8[6291456]{0:T(1024)(128)(4,1)} %bitcast.472), calls=%async_computation.6 | async-start | bytes 4194304
  165.9 4.4 %copy-start.6 = (bf16[1,16,8,128,128]{4,3,0,1,2:T(8,128)(2,1)S(1)}, bf16[1,16,8,128,128]{4,3,0,1,2:T(8,128)(2,1)}, u32[]{:S(2)}) copy-start(bf16[1,16,8,128,128]{4,3,0,1,2:T(8,128)(2,1)} %get-tuple-element.29) | copy-start | bytes 12582916
  188.2 4.5 %copy-start.5 = (bf16[16,8,128,128]{3,2,0,1:T(8,128)(2,1)S(1)}, bf16[16,8,128,128]{3,2,0,1:T(8,128)(2,1)}, u32[]{:S(2)}) copy-start(bf16[16,8,128,128]{3,2,0,1:T(8,128)(2,1)} %get-tuple-element.24) | copy-start | bytes 12582916
  207.2 8.9 %copy-start.3 = (f32[16,128,8,128]{3,1,2,0:T(8,128)S(1)}, f32[16,128,8,128]{3,1,2,0:T(8,128)}, u32[]{:S(2)}) copy-start(f32[16,128,8,128]{3,1,2,0:T(8,128)} %fusion.20) | copy-start | bytes 25165828
  212.3 30.3 %collective-permute-start.6 = (bf16[2,4,8,128,128]{4,3,0,1,2:T(8,128)(2,1)}, bf16[2,4,8,128,128]{4,3,0,1,2:T(8,128)(2,1)S(1)}, u32[]{:S(2)}, u32[]{:S(2)}) collective-permute-start(bf16[2,4,8,128,128]{4,3,0,1,2:T(8,128)(2,1)} %get-tuple-element.42), channel_id=1, source_target_pairs={{0,8},{8,16},{16,24},{24,32},{32,40},{40,48},{48,56},{56,64},{64,7... | collective-permute-start | bytes 6291464 | tf_op jit(solution)/shard_map/ppermute | solution.py:12
  216.1 22.5 %copy-start.2 = (bf16[2,8,1024,128]{3,2,0,1:T(8,128)(2,1)S(1)}, bf16[2,8,1024,128]{3,2,0,1:T(8,128)(2,1)}, u32[]{:S(2)}) copy-start(bf16[2,8,1024,128]{3,2,0,1:T(8,128)(2,1)} %all-gather.6.cloned.1.call-done) | copy-start | bytes 12582916
  236.2 4.9 %copy-start.4 = (bf16[16,128,8,128]{3,1,2,0:T(8,128)(2,1)S(1)}, bf16[16,128,8,128]{3,1,2,0:T(8,128)(2,1)}, u32[]{:S(2)}) copy-start(bf16[16,128,8,128]{3,1,2,0:T(8,128)(2,1)} %select_convert_fusion) | copy-start | bytes 12582916
  236.2 27.8 %collective-permute-start.7 = (bf16[2,4,8,128,128]{4,3,0,1,2:T(8,128)(2,1)}, bf16[2,4,8,128,128]{4,3,0,1,2:T(8,128)(2,1)S(1)}, u32[]{:S(2)}, u32[]{:S(2)}) collective-permute-start(bf16[2,4,8,128,128]{4,3,0,1,2:T(8,128)(2,1)} %get-tuple-element.41), channel_id=1, source_target_pairs={{8,0},{16,8},{24,16},{32,24},{40,32},{48,40},{56,48},{64,56},{72,6... | collective-permute-start | bytes 6291464 | tf_op jit(solution)/shard_map/ppermute | solution.py:15
  265.8 1.0 copy-start.8
  267.3 0.8 copy-start.9
  319.3 12.6 %all-to-all-start.2 = ((f32[32,1,2,96]{3,2,1,0:T(2,128)}), f32[32,1,2,96]{3,2,1,0:T(2,128)S(1)}, u32[]{:S(2)}, u32[]{:S(2)}) async-start(f32[32,1,2,96]{3,2,1,0:T(2,128)} %broadcast_in_dim.170), calls=%async_computation.2 | async-start | bytes 65536 | tf_op jit(solution)/shard_map/all_to_all | solution.py:22
Sparse Core Ops, SparseCore 0:
  11.7 78.2 all-gather.3
  152.8 54.4 all-gather.5
where the time goes:
time: 343 us; the launch traced here: 342 us
  waiting for transfers between devices  126 us (37%)
  matrix products  69.8 us (20%)
  blocking collectives  47.2 us (14%)
  local copies, waits for them, and re-layouts  45.7 us (13%)
  starting transfers between devices  29 us (8%)
  between operations  15.5 us (5%)
  other arithmetic  8.87 us (3%)
    all_gather x1, waiting for transfers between devices, on_device(): whole_rows = lax.all_gather(stacked, 'orb', axis=2, tiled=True)  78.4 us
    dot_general x8, matrix products, all_slot_product(): jnp.matmul(factor_left[:, :, stride:stride + 1], source, preferred_elemen...  52.8 us
    all_to_all x2, blocking collectives, sent_to_all(): return lax.all_to_all(copies, axis, split_axis=0, concat_axis=0, tiled=True)  47.2 us
    ppermute x4, waiting for transfers between devices, padded_2(): lax.ppermute(lax.slice_in_dim(block, 0, width, axis=dim), axis, backward)  27.4 us
    ppermute x4, starting transfers between devices, padded_2(): lax.ppermute(lax.slice_in_dim(block, block.shape[dim] - width, None, axis...  15 us
    dot_general x32, matrix products, own_slot_product(): jnp.matmul(factor_left[:, :, stride], picked, preferred_element_type=jnp....  13.2 us
    unnamed x50, local copies, waits for them, and re-layouts  13.2 us
    slice x1, local copies, waits for them, and re-layouts, all_slot_product(): right_rims[:, stride:stride + count_rows]  11 us
  transfers between devices with their start and end apart: 11, of which 9 were waited for; matrix products, arithmetic and copies ran while one was open for 27% of the time, Pallas kernels for 0%

commit v1 on v0

--- a/solution.py
+++ b/solution.py
@@ -2,6 +2,13 @@
 import jax.numpy as jnp
 from jax import lax
 from jax.sharding import PartitionSpec as P
+
+
+def exchange_gather(x, axis, along):
+    devices = lax.axis_size(axis)
+    blocks = jnp.stack([x for _ in range(devices)])
+    blocks = lax.all_to_all(blocks, axis, split_axis=0, concat_axis=0)
+    return jnp.concatenate(blocks, axis=along)
 
 
 def padded_2(block, sides, width):
@@ -116,7 +123,7 @@
     density = jnp.where(keep_own, density_in[None], zero_half)
     perturbed = jnp.where(keep_own, field_terms, zero_half)
     stacked = jnp.concatenate([density, perturbed], 0)
-    whole_rows = lax.all_gather(stacked, "orb", axis=2, tiled=True)
+    whole_rows = exchange_gather(stacked, "orb", 2)
     deep_rows = padded_2(whole_rows[0:1], (("aux", 1),), 2 * half_band)
     field_rows = rim_fields(whole_rows[1:], half_band)
     pattern_wide = padded_2(band_pattern, (("aux", 0),), half_band)

time: 343 us -> 422 us (1.23)
  blocking collectives: 47.2 us -> 196 us
  waiting for transfers between devices: 126 us -> 53.4 us
  local copies, waits for them, and re-layouts: 45.7 us -> 38.7 us
  matrix products: 69.8 us -> 76.4 us
    all_to_all x0 -> x1, blocking collectives: none -> 148 us  [exchange_gather(): blocks = lax.all_to_all(blocks, axis, split_axis=0, concat_axis=0)]
    all_gather x1 -> x0, waiting for transfers between devices: 78.4 us -> none  [on_device(): whole_rows = lax.all_gather(stacked, 'orb', axis=2, tiled=True)]
    dot_general x32, matrix products: 13.2 us -> 19.8 us  [own_slot_product(): jnp.matmul(factor_left[:, :, stride], picked, preferred_element_type=jnp....]
    unnamed x50 -> x33, local copies, waits for them, and re-layouts: 13.2 us -> 8.05 us
  transfers between devices with their start and end apart: 11 -> 10, of which waited for: 9 -> 8; matrix products, arithmetic and copies ran while one was open for 27% -> 20% of each run, Pallas kernels for 0% -> 0%
where the time goes in v1:
time: 422 us; the launch traced here: 421 us
  blocking collectives  196 us (46%)
  matrix products  76.4 us (18%)
  waiting for transfers between devices  53.4 us (13%)
  local copies, waits for them, and re-layouts  38.7 us (9%)
  starting transfers between devices  29.1 us (7%)
  between operations  15.4 us (4%)
  other arithmetic  12.2 us (3%)
    all_to_all x1, blocking collectives, exchange_gather(): blocks = lax.all_to_all(blocks, axis, split_axis=0, concat_axis=0)  148 us
    dot_general x8, matrix products, all_slot_product(): jnp.matmul(factor_left[:, :, stride:stride + 1], source, preferred_elemen...  52.8 us
    all_to_all x2, blocking collectives, sent_to_all(): return lax.all_to_all(copies, axis, split_axis=0, concat_axis=0, tiled=True)  47.2 us
    ppermute x4, waiting for transfers between devices, padded_2(): lax.ppermute(lax.slice_in_dim(block, 0, width, axis=dim), axis, backward)  30.9 us
    dot_general x32, matrix products, own_slot_product(): jnp.matmul(factor_left[:, :, stride], picked, preferred_element_type=jnp....  19.8 us
    ppermute x4, starting transfers between devices, padded_2(): lax.ppermute(lax.slice_in_dim(block, block.shape[dim] - width, None, axis...  14.8 us
    ppermute x4, waiting for transfers between devices, padded_2(): lax.ppermute(lax.slice_in_dim(block, block.shape[dim] - width, None, axis...  12.9 us
    slice x1, local copies, waits for them, and re-layouts, all_slot_product(): right_rims[:, stride:stride + count_rows]  10.6 us
  transfers between devices with their start and end apart: 10, of which 8 were waited for; matrix products, arithmetic and copies ran while one was open for 20% of the time, Pallas kernels for 0%

profile of v1, /device:TPU:1, one launch (start us, length us, event | category | flops | bytes accessed | tf_op | source)
XLA Modules:
  0.0 420.7 jit_solution(14130313957078165435)
XLA Ops:
  10.6 1.6 stack.2
  12.3 148.4 %all_to_all.20 = bf16[8,3,8,1,128,128]{5,4,1,2,3,0:T(8,128)(2,1)S(1)} all-to-all(bf16[8,3,8,1,128,128]{5,4,1,2,3,0:T(8,128)(2,1)S(1)} %stack.2), channel_id=1, replica_groups=mesh['aux'=32,'orb'=8] {'orb'}, dimensions={0} | all-to-all | bytes 12582912 | tf_op jit(solution)/shard_map/all_to_all | solution.py:10
  160.7 1.5 slice_bitcast_fusion.1
  162.2 5.4 %collective-permute-start.2 = (bf16[1,8,8,128,128]{4,3,1,2,0:T(8,128)(2,1)}, bf16[1,8,8,128,128]{4,3,1,2,0:T(8,128)(2,1)}, u32[]{:S(2)}, u32[]{:S(2)}) collective-permute-start(bf16[1,8,8,128,128]{4,3,1,2,0:T(8,128)(2,1)} %slice_bitcast_fusion.1), channel_id=1, source_target_pairs={{0,8},{8,16},{16,24},{24,32},{32,40},{40,48},{48,56},{56,64},{64,7... | collective-permute-start | bytes 6291464 | tf_op jit(solution)/shard_map/ppermute | solution.py:19
  167.6 1.9 collective-permute-start.3
  170.1 2.4 fusion.316
  173.6 3.6 collective-permute-start
  177.3 2.1 collective-permute-start.1
  179.4 11.5 %collective-permute-done.2 = bf16[1,8,8,128,128]{4,3,1,2,0:T(8,128)(2,1)} collective-permute-done((bf16[1,8,8,128,128]{4,3,1,2,0:T(8,128)(2,1)}, bf16[1,8,8,128,128]{4,3,1,2,0:T(8,128)(2,1)}, u32[]{:S(2)}, u32[]{:S(2)}) %collective-permute-start.2) | collective-permute-done | bytes 2097184 | tf_op jit(solution)/shard_map/ppermute | solution.py:19
  190.9 4.4 %collective-permute-done.3 = bf16[1,8,8,128,128]{4,3,1,2,0:T(8,128)(2,1)} collective-permute-done((bf16[1,8,8,128,128]{4,3,1,2,0:T(8,128)(2,1)}, bf16[1,8,8,128,128]{4,3,1,2,0:T(8,128)(2,1)}, u32[]{:S(2)}, u32[]{:S(2)}) %collective-permute-start.3) | collective-permute-done | bytes 2097184 | tf_op jit(solution)/shard_map/ppermute | solution.py:22
  195.3 3.7 pad_maximum_fusion.1
  199.0 10.6 %fusion.314 = (bf16[1,16,8,128,128]{4,3,1,2,0:T(8,128)(2,1)}, bf16[16,8,128,128]{3,2,0,1:T(8,128)(2,1)}, bf16[1,16,8,128,128]{4,3,1,2,0:T(8,128)(2,1)}, bf16[1,1...) fusion(bf16[1,24,8,128,128]{4,3,1,2,0:T(8,128)(2,1)S(1)} %pad_m, ...), kind=kLoop, calls=%fused_computation.404 | loop fusion | bytes 62914560 | tf_op jit(solution)/shard_map/slice | solution.py:100
  209.6 1.8 copy-done.1
  212.0 1.4 collective-permute-done
  213.4 4.4 %collective-permute-done.1 = bf16[2,4,8,128,128]{4,3,0,1,2:T(8,128)(2,1)} collective-permute-done((bf16[2,4,8,128,128]{4,3,0,1,2:T(8,128)(2,1)}, bf16[2,4,8,128,128]{4,3,0,1,2:T(8,128)(2,1)}, u32[]{:S(2)}, u32[]{:S(2)}) %collective-permute-start.1) | collective-permute-done | bytes 2097184 | tf_op jit(solution)/shard_map/ppermute | solution.py:22
  217.8 3.3 pad_maximum_fusion
  222.3 1.2 convolution_add_fusion.27
  223.9 1.2 convolution_add_fusion.26
  225.4 1.2 convolution_add_fusion.25
  228.5 1.2 convolution_add_fusion.23
  231.3 1.2 fusion.38
  233.7 1.9 collective-permute-start.4
  235.6 2.6 collective-permute-start.5
  238.9 1.6 collective-permute-done.5
  240.6 3.7 fusion.4
  244.9 3.4 fusion.2
  249.3 4.3 %fusion.22 = f32[16,128,8,128]{3,1,2,0:T(8,128)} fusion(bf16[1,24,8,128,128]{4,3,1,2,0:T(8,128)(2,1)S(1)} %bitcast.468, bf16[1,16,8,128,128]{4,3,1,2,0:T(8,128)(2,1)S(1)} %copy-done.8), kind=kOutput, calls=%fused_computation.33 | convolution fusion | flops 536870912 | bytes 13107200 | tf_op jit(solution)/shard_map/dot_general | solution.py:101
  253.6 4.5 %fusion.20 = f32[16,128,8,128]{3,1,2,0:T(8,128)} fusion(bf16[16,8,128,128]{3,2,0,1:T(8,128)(2,1)S(1)} %get-tuple-element.39, bf16[1,24,8,128,128]{4,3,1,2,0:T(8,128)(2,1)S(1)} %bitcast.468), kind=kOutput, calls=%fused_computation.31 | convolution fusion | flops 536870912 | bytes 13107200 | tf_op jit(solution)/shard_map/dot_general | solution.py:101
  258.1 4.5 %fusion.18 = f32[16,128,8,128]{3,1,2,0:T(8,128)} fusion(bf16[16,8,128,128]{3,2,0,1:T(8,128)(2,1)S(1)} %get-tuple-element.37, bf16[1,24,8,128,128]{4,3,1,2,0:T(8,128)(2,1)S(1)} %bitcast.468), kind=kOutput, calls=%fused_computation.29 | convolution fusion | flops 536870912 | bytes 13107200 | tf_op jit(solution)/shard_map/dot_general | solution.py:101
  262.6 4.5 %fusion.14 = f32[16,128,8,128]{3,1,2,0:T(8,128)} fusion(bf16[16,8,128,128]{3,2,0,1:T(8,128)(2,1)S(1)} %get-tuple-element.38, bf16[1,24,8,128,128]{4,3,1,2,0:T(8,128)(2,1)S(1)} %bitcast.468), kind=kOutput, calls=%fused_computation.25 | convolution fusion | flops 536870912 | bytes 13107200 | tf_op jit(solution)/shard_map/dot_general | solution.py:101
  267.1 4.5 %fusion.12 = f32[16,128,8,128]{3,1,2,0:T(8,128)} fusion(bf16[16,8,128,128]{3,2,0,1:T(8,128)(2,1)S(1)} %get-tuple-element.40, bf16[1,24,8,128,128]{4,3,1,2,0:T(8,128)(2,1)S(1)} %bitcast.468), kind=kOutput, calls=%fused_computation.23 | convolution fusion | flops 536870912 | bytes 13107200 | tf_op jit(solution)/shard_map/dot_general | solution.py:101
  271.6 4.5 %fusion.16 = f32[16,128,8,128]{3,1,2,0:T(8,128)} fusion(bf16[16,8,128,128]{3,2,0,1:T(8,128)(2,1)S(1)} %copy-done.7, bf16[1,24,8,128,128]{4,3,1,2,0:T(8,128)(2,1)S(1)} %bitcast.468), kind=kOutput, calls=%fused_computation.27 | convolution fusion | flops 536870912 | bytes 13107200 | tf_op jit(solution)/shard_map/dot_general | solution.py:101
  276.1 5.9 %fusion.24 = f32[16,128,8,128]{3,1,2,0:T(8,128)} fusion(bf16[1,24,8,128,128]{4,3,1,2,0:T(8,128)(2,1)S(1)} %bitcast.468, bf16[1,8,8,128,128]{4,3,1,2,0:T(8,128)(2,1)} %slice_bitcast_fusion.1, bf16[1,8,8,128,128]{4,3,1,2,0:T(8,128)(2,1)} %collective-permute-done.2), kind=kOutput, calls=%fused_computation.35 | convolution fusion | flops 553648128 | bytes 13107200 | tf_op jit(solution)/shard_map/dot_general | solution.py:101
  281.9 4.1 all-gather.3.cloned.1.call-done
  286.1 5.1 %fusion.315 = (bf16[2,4,8,128,128]{4,3,0,1,2:T(8,128)(2,1)}, bf16[2,4,8,128,128]{4,3,0,1,2:T(8,128)(2,1)}) fusion(bf16[2,8,8,128,128]{4,3,2,0,1:T(8,128)(2,1)} %bitcast.469), kind=kLoop, calls=%fused_computation.405 | loop fusion | bytes 8388608 | tf_op jit(solution)/shard_map/slice | solution.py:22
  291.1 3.8 collective-permute-start.6
  294.9 20.2 %select_convert_fusion = bf16[16,128,8,128]{3,1,2,0:T(8,128)(2,1)} fusion(f32[16,128,8,128]{3,1,2,0:T(8,128)S(1)} %copy-done.5, f32[16,128,8,128]{3,1,2,0:T(8,128)} %fusion.14, f32[16,128,8,128]{3,1,2,0:T(8,128)} %fusion.16, f32[16,128,8,128]{3,1,2,0:T(8,128)} %fusion.18, f32[16,128,8,128]{3,1,2,0:T(8,128)} %fusion.20, f32[16,128,8,128]{3,1,2,0:T(8,128)} %fusion.24, ...), kind=kOutput, calls=%fused_computation.4 | convolution fusion | flops 555745280 | bytes 67633280 | tf_op jit(solution)/shard_map/dot_general | solution.py:101
  315.1 2.4 collective-permute-start.7
  317.5 1.2 fusion.46
  318.8 1.2 convolution_add_fusion.6
  322.4 20.5 %collective-permute-done.7 = bf16[2,4,8,128,128]{4,3,0,1,2:T(8,128)(2,1)S(1)} collective-permute-done((bf16[2,4,8,128,128]{4,3,0,1,2:T(8,128)(2,1)}, bf16[2,4,8,128,128]{4,3,0,1,2:T(8,128)(2,1)S(1)}, u32[]{:S(2)}, u32[]{:S(2)}) %collective-permute-start.7) | collective-permute-done | bytes 2097184 | tf_op jit(solution)/shard_map/ppermute | solution.py:22
  347.5 36.8 %all_to_all.21 = bf16[32,2,1,1,128,128]{5,4,3,2,1,0:T(8,128)(2,1)} all-to-all(bf16[32,2,1,1,128,128]{5,4,3,2,1,0:T(8,128)(2,1)S(1)} %broadcast_in_dim.168), channel_id=1, replica_groups=mesh['aux'=32,'orb'=8] {'aux'}, dimensions={0} | all-to-all | bytes 4194304 | tf_op jit(solution)/shard_map/all_to_all | solution.py:29
  384.3 1.9 reduce_sum.21
  387.2 10.4 %all_to_all.22 = f32[8,1,2,96]{3,2,1,0:T(2,128)S(1)} all-to-all(f32[8,1,2,96]{3,2,1,0:T(2,128)S(1)} %broadcast_in_dim.169), channel_id=1, replica_groups=mesh['aux'=32,'orb'=8] {'orb'}, dimensions={0} | all-to-all | bytes 12288 | tf_op jit(solution)/shard_map/all_to_all | solution.py:29
  398.2 5.3 %all-to-all-start.3 = ((f32[32,1,2,96]{3,2,1,0:T(2,128)}), f32[32,1,2,96]{3,2,1,0:T(2,128)S(1)}, u32[]{:S(2)}, u32[]{:S(2)}) async-start(f32[32,1,2,96]{3,2,1,0:T(2,128)} %broadcast_in_dim.170), calls=%async_computation.3 | async-start | bytes 65536 | tf_op jit(solution)/shard_map/all_to_all | solution.py:29
  403.6 1.9 copy.117
  405.4 5.5 %all-to-all-done.3 = f32[32,1,2,96]{3,2,1,0:T(2,128)S(1)} async-done(((f32[32,1,2,96]{3,2,1,0:T(2,128)}), f32[32,1,2,96]{3,2,1,0:T(2,128)S(1)}, u32[]{:S(2)}, u32[]{:S(2)}) %all-to-all-start.3) | async-done | bytes 24608 | tf_op jit(solution)/shard_map/all_to_all | solution.py:29
  411.0 2.9 fusion.43
  (80 shorter events, 22.0 us)
Async XLA Ops:
  7.2 379.1 %copy-start = (bf16[1,96,1,16384]{3,1,2,0:T(8,128)(2,1)S(1)}, bf16[1,96,1,16384]{3,1,2,0:T(8,128)(2,1)}, u32[]{:S(2)}) copy-start(bf16[1,96,1,16384]{3,1,2,0:T(8,128)(2,1)} %param.10) | copy-start | bytes 9437188
  7.2 278.9 %all-gather.3.cloned.1.call-start = ((), (), s32[]{:S(2)}) async-start(), calls=%async_computation.4 | async-start | bytes 4718592 | tf_op jit(solution)/shard_map/all_gather | solution.py:138
  162.2 28.7 %collective-permute-start.2 = (bf16[1,8,8,128,128]{4,3,1,2,0:T(8,128)(2,1)}, bf16[1,8,8,128,128]{4,3,1,2,0:T(8,128)(2,1)}, u32[]{:S(2)}, u32[]{:S(2)}) collective-permute-start(bf16[1,8,8,128,128]{4,3,1,2,0:T(8,128)(2,1)} %slice_bitcast_fusion.1), channel_id=1, source_target_pairs={{0,8},{8,16},{16,24},{24,32},{32,40},{40,48},{48,56},{56,64},{64,7... | collective-permute-start | bytes 6291464 | tf_op jit(solution)/shard_map/ppermute | solution.py:19
  167.6 27.7 %collective-permute-start.3 = (bf16[1,8,8,128,128]{4,3,1,2,0:T(8,128)(2,1)}, bf16[1,8,8,128,128]{4,3,1,2,0:T(8,128)(2,1)}, u32[]{:S(2)}, u32[]{:S(2)}) collective-permute-start(bf16[1,8,8,128,128]{4,3,1,2,0:T(8,128)(2,1)} %slice_bitcast_fusion.1), channel_id=1, source_target_pairs={{8,0},{16,8},{24,16},{32,24},{40,32},{48,40},{56,48},{64,56},{72,6... | collective-permute-start | bytes 6291464 | tf_op jit(solution)/shard_map/ppermute | solution.py:22
  170.1 3.5 copy-start.2
  173.6 39.7 %collective-permute-start = (bf16[2,4,8,128,128]{4,3,0,1,2:T(8,128)(2,1)}, bf16[2,4,8,128,128]{4,3,0,1,2:T(8,128)(2,1)}, u32[]{:S(2)}, u32[]{:S(2)}) collective-permute-start(bf16[2,4,8,128,128]{4,3,0,1,2:T(8,128)(2,1)} %get-tuple-element.33), channel_id=1, source_target_pairs={{0,8},{8,16},{16,24},{24,32},{32,40},{40,48},{48,56},{56,64},{64,7... | collective-permute-start | bytes 6291464 | tf_op jit(solution)/shard_map/ppermute | solution.py:19
  177.3 40.5 %collective-permute-start.1 = (bf16[2,4,8,128,128]{4,3,0,1,2:T(8,128)(2,1)}, bf16[2,4,8,128,128]{4,3,0,1,2:T(8,128)(2,1)}, u32[]{:S(2)}, u32[]{:S(2)}) collective-permute-start(bf16[2,4,8,128,128]{4,3,0,1,2:T(8,128)(2,1)} %get-tuple-element.34), channel_id=1, source_target_pairs={{8,0},{16,8},{24,16},{32,24},{40,32},{48,40},{56,48},{64,56},{72,6... | collective-permute-start | bytes 6291464 | tf_op jit(solution)/shard_map/ppermute | solution.py:22
  199.0 12.5 %copy-start.1 = (bf16[1,24,8,128,128]{4,3,1,2,0:T(8,128)(2,1)}, bf16[1,24,8,128,128]{4,3,1,2,0:T(8,128)(2,1)S(1)}, u32[]{:S(2)}) copy-start(bf16[1,24,8,128,128]{4,3,1,2,0:T(8,128)(2,1)S(1)} %pad_maximum_fusion.1) | copy-start | bytes 18874372
  199.0 12.4 %copy-start.3 = (bf16[2,8,8,128,128]{4,3,0,1,2:T(8,128)(2,1)S(1)}, bf16[2,8,8,128,128]{4,3,0,1,2:T(8,128)(2,1)}, u32[]{:S(2)}) copy-start(bf16[2,8,8,128,128]{4,3,0,1,2:T(8,128)(2,1)} %copy-done.2) | copy-start | bytes 12582916
  230.1 3.6 copy-start.12
  233.7 5.2 %collective-permute-start.4 = (s32[4,8]{1,0:T(4,128)S(1)}, s32[4,8]{1,0:T(4,128)S(1)}, u32[]{:S(2)}, u32[]{:S(2)}) collective-permute-start(s32[4,8]{1,0:T(4,128)S(1)} %get-tuple-element.35), channel_id=1, source_target_pairs={{0,8},{8,16},{16,24},{24,32},{32,40},{40,48},{48,56},{56,64},{64,7... | collective-permute-start | bytes 392 | tf_op jit(solution)/shard_map/ppermute | solution.py:19
  235.6 4.9 %collective-permute-start.5 = (s32[4,8]{1,0:T(4,128)S(1)}, s32[4,8]{1,0:T(4,128)S(1)}, u32[]{:S(2)}, u32[]{:S(2)}) collective-permute-start(s32[4,8]{1,0:T(4,128)S(1)} %get-tuple-element.36), channel_id=1, source_target_pairs={{8,0},{16,8},{24,16},{32,24},{40,32},{48,40},{56,48},{64,56},{72,6... | collective-permute-start | bytes 392 | tf_op jit(solution)/shard_map/ppermute | solution.py:22
  240.6 4.2 %copy-start.9 = (bf16[1,16,8,128,128]{4,3,1,2,0:T(8,128)(2,1)S(1)}, bf16[1,16,8,128,128]{4,3,1,2,0:T(8,128)(2,1)}, u32[]{:S(2)}) copy-start(bf16[1,16,8,128,128]{4,3,1,2,0:T(8,128)(2,1)} %get-tuple-element.26) | copy-start | bytes 12582916
  240.6 7.6 %slice-start = ((s8[6291456]{0:T(1024)(128)(4,1)}), s8[4194304]{0:T(1024)(128)(4,1)S(1)}, s32[]{:S(2)}) async-start(s8[6291456]{0:T(1024)(128)(4,1)} %bitcast.467), calls=%async_computation.5 | async-start | bytes 8388608
  244.4 4.9 %slice-start.1 = ((s8[6291456]{0:T(1024)(128)(4,1)}), s8[2097152]{0:T(1024)(128)(4,1)S(1)}, s32[]{:S(2)}) async-start(s8[6291456]{0:T(1024)(128)(4,1)} %bitcast.467), calls=%async_computation.6 | async-start | bytes 4194304
  244.9 4.4 %copy-start.8 = (bf16[1,16,8,128,128]{4,3,1,2,0:T(8,128)(2,1)S(1)}, bf16[1,16,8,128,128]{4,3,1,2,0:T(8,128)(2,1)}, u32[]{:S(2)}) copy-start(bf16[1,16,8,128,128]{4,3,1,2,0:T(8,128)(2,1)} %get-tuple-element.29) | copy-start | bytes 12582916
  267.1 4.5 %copy-start.7 = (bf16[16,8,128,128]{3,2,0,1:T(8,128)(2,1)S(1)}, bf16[16,8,128,128]{3,2,0,1:T(8,128)(2,1)}, u32[]{:S(2)}) copy-start(bf16[16,8,128,128]{3,2,0,1:T(8,128)(2,1)} %get-tuple-element.24) | copy-start | bytes 12582916
  286.0 8.9 %copy-start.5 = (f32[16,128,8,128]{3,1,2,0:T(8,128)S(1)}, f32[16,128,8,128]{3,1,2,0:T(8,128)}, u32[]{:S(2)}) copy-start(f32[16,128,8,128]{3,1,2,0:T(8,128)} %fusion.12) | copy-start | bytes 25165828
  291.1 30.4 %collective-permute-start.6 = (bf16[2,4,8,128,128]{4,3,0,1,2:T(8,128)(2,1)}, bf16[2,4,8,128,128]{4,3,0,1,2:T(8,128)(2,1)S(1)}, u32[]{:S(2)}, u32[]{:S(2)}) collective-permute-start(bf16[2,4,8,128,128]{4,3,0,1,2:T(8,128)(2,1)} %get-tuple-element.32), channel_id=1, source_target_pairs={{0,8},{8,16},{16,24},{24,32},{32,40},{40,48},{48,56},{56,64},{64,7... | collective-permute-start | bytes 6291464 | tf_op jit(solution)/shard_map/ppermute | solution.py:19
  294.9 22.6 %copy-start.4 = (bf16[2,8,1024,128]{3,2,0,1:T(8,128)(2,1)S(1)}, bf16[2,8,1024,128]{3,2,0,1:T(8,128)(2,1)}, u32[]{:S(2)}) copy-start(bf16[2,8,1024,128]{3,2,0,1:T(8,128)(2,1)} %all-gather.3.cloned.1.call-done) | copy-start | bytes 12582916
  315.1 4.9 %copy-start.6 = (bf16[16,128,8,128]{3,1,2,0:T(8,128)(2,1)S(1)}, bf16[16,128,8,128]{3,1,2,0:T(8,128)(2,1)}, u32[]{:S(2)}) copy-start(bf16[16,128,8,128]{3,1,2,0:T(8,128)(2,1)} %select_convert_fusion) | copy-start | bytes 12582916
  315.1 27.8 %collective-permute-start.7 = (bf16[2,4,8,128,128]{4,3,0,1,2:T(8,128)(2,1)}, bf16[2,4,8,128,128]{4,3,0,1,2:T(8,128)(2,1)S(1)}, u32[]{:S(2)}, u32[]{:S(2)}) collective-permute-start(bf16[2,4,8,128,128]{4,3,0,1,2:T(8,128)(2,1)} %get-tuple-element.31), channel_id=1, source_target_pairs={{8,0},{16,8},{24,16},{32,24},{40,32},{48,40},{56,48},{64,56},{72,6... | collective-permute-start | bytes 6291464 | tf_op jit(solution)/shard_map/ppermute | solution.py:22
  344.7 1.0 copy-start.10
  346.2 0.8 copy-start.11
  398.2 12.7 %all-to-all-start.3 = ((f32[32,1,2,96]{3,2,1,0:T(2,128)}), f32[32,1,2,96]{3,2,1,0:T(2,128)S(1)}, u32[]{:S(2)}, u32[]{:S(2)}) async-start(f32[32,1,2,96]{3,2,1,0:T(2,128)} %broadcast_in_dim.170), calls=%async_computation.3 | async-start | bytes 65536 | tf_op jit(solution)/shard_map/all_to_all | solution.py:29
Sparse Core Ops, SparseCore 0:
  233.8 52.1 all-gather.2
